TPU v7x, 32 devices: a whole 2x2x4 slice. The times are simulated.
32 devices in a mesh: expert: 2 (over y), blk: 16 (over z, x, core).
Axes of the slice: x: 2, y: 2, z: 4, core: 2. Of those that a mesh axis runs over, the one named last changes fastest.
Arguments:
- query_grads: bfloat16 [2, 16384, 2304], P('expert', 'blk'), may hold values from -0.125 to 0.125
- train_grads: bfloat16 [2, 128, 2304], P('expert', 'blk'), may hold values from -6 to 6
- counts: int32 [2, 128], P('expert', 'blk'), may hold values from 0 to 64
- factor: bfloat16 [2, 2304, 2304], P('expert', 'blk'), as said below
Outputs:
- scores: float32 [16384, 128], P('blk', 'expert')
Inputs may be any that keep to these rules, and one draw needn't show every extreme that they name: counts of tokens of one example, 0 where the expert gets none of them. Each expert's factor has the largest entry of each row on its diagonal.
All inputs are finite; a program needn't handle non-finite values.
Results may differ from a plain program's by a relative error of at most 0.0038.
Values may be sent and summed in bfloat16 or wider, within the bound.
A program may use at most 64 MiB of HBM per device.

v0:
```python
import jax
import jax.numpy as jnp
from jax import lax
from jax.sharding import PartitionSpec as P

TOKS_EX = 64


def on_device(query_grads, train_grads, counts, factor):
    full_factor = lax.all_gather(factor, "blk", axis=1, tiled=True)
    pre_train = jnp.einsum(
        "etr,erk->etk", train_grads, full_factor, preferred_element_type=jnp.float32
    ).astype(jnp.bfloat16)
    kernel = jnp.einsum(
        "etk,erk->etr", pre_train, full_factor, preferred_element_type=jnp.float32
    ).astype(jnp.bfloat16)
    kernel_piece = lax.all_gather(kernel, "blk", axis=1, tiled=True)
    count_piece = lax.all_gather(counts, "blk", axis=1, tiled=True)
    products = jnp.einsum(
        "eqk,etk->eqt", query_grads, kernel_piece, preferred_element_type=jnp.float32
    )
    weights = count_piece.astype(jnp.float32) / TOKS_EX
    score_block = jnp.sum(products * weights[:, None, :], axis=0)
    return lax.psum_scatter(score_block, "expert", scatter_dimension=1, tiled=True)


def solution(mesh):
    return jax.shard_map(
        on_device,
        mesh=mesh,
        in_specs=(
            P("expert", "blk", None),
            P("expert", "blk", None),
            P("expert", "blk"),
            P("expert", "blk", None),
        ),
        out_specs=P("blk", "expert"),
        check_vma=False,
    )
```

profile of v0, /device:TPU:0, one launch (start us, length us, event | category | flops | bytes accessed | tf_op | source)
XLA Modules:
  0.0 156.0 jit_solution(9848511211916977124)
XLA Ops:
  6.5 0.0 copy-start
  6.5 0.0 all-gather.3.cloned.1.call-start
  6.5 0.7 all-gather.3.cloned.1.call-update
  7.3 0.0 reduce-scatter.2.cloned.1.call-start
  7.3 1.2 dynamic-slice
  9.2 0.8 bitcast_dynamic-update-slice_fusion
  10.0 13.8 %all-reduce = s32[128]{0:T(128)S(1)} all-reduce(s32[128]{0:T(128)S(1)} %bitcast_dynamic-update-slice_fusion), channel_id=1, replica_groups=mesh['expert'=2,'blk'=16] {'blk'}, use_global_device_ids=true, to_apply=%add | all-reduce | flops 128 | bytes 1024
  23.8 76.9 %all-gather.3.cloned.1.call-done = bf16[1,2304,2304]{2,1,0:T(8,128)(2,1)} async-done(((bf16[1,144,2304]{2,1,0:T(8,128)(2,1)}), bf16[1,2304,2304]{2,1,0:T(8,128)(2,1)}) %all-gather.3.cloned.1.call-update) | async-done | bytes 10616848 | tf_op jit(solution)/shard_map/all_gather | solution.py:10
  100.7 0.0 copy-done
  100.7 11.3 %fusion.9 = bf16[8,2304]{1,0:T(8,128)(2,1)S(1)} fusion(bf16[1,2304,2304]{2,1,0:T(8,128)(2,1)} %all-gather.3.cloned.1.call-done, bf16[1,8,2304]{2,1,0:T(8,128)(2,1)S(1)} %copy-done), kind=kOutput, calls=%fused_computation.7 | convolution fusion | flops 169906176 | bytes 10690560 | tf_op jit(solution)/shard_map/etk,erk->etr/dot_general | solution.py:14
  112.0 20.3 %all-gather = bf16[128,2304]{1,0:T(8,128)(2,1)S(1)} all-gather(bf16[8,2304]{1,0:T(8,128)(2,1)S(1)} %fusion.9), channel_id=2, replica_groups=mesh['expert'=2,'blk'=16] {'blk'}, dimensions={0}, use_global_device_ids=true | all-gather | bytes 626688 | tf_op jit(solution)/shard_map/all_gather | solution.py:17
  132.3 4.7 %fusion.17 = f32[1024,128]{0,1:T(8,128)} fusion(bf16[128,2304]{1,0:T(8,128)(2,1)S(1)} %all-gather, bf16[1,1024,2304]{2,1,0:T(8,128)(2,1)} %param.4, f32[128]{0:T(128)S(1)} %convert_multiply_fusion), kind=kOutput, calls=%fused_computation.9 | convolution fusion | flops 604110848 | bytes 5833216 | tf_op jit(solution)/shard_map/eqk,etk->eqt/dot_general | solution.py:19
  137.1 0.0 reduce-scatter.2.cloned.1.call-update
  137.1 12.0 %reduce-scatter.2.cloned.1.call-done = f32[1024,64]{0,1:T(8,128)} async-done(((f32[1024,128]{0,1:T(8,128)}), f32[1024,64]{0,1:T(8,128)}) %reduce-scatter.2.cloned.1.call-update) | async-done | bytes 262160 | tf_op jit(solution)/shard_map/reduce_scatter | solution.py:24
  (2 shorter events, 0.0 us)
Async XLA Ops:
  6.5 94.2 %copy-start = (bf16[1,8,2304]{2,1,0:T(8,128)(2,1)S(1)}, bf16[1,8,2304]{2,1,0:T(8,128)(2,1)}, u32[]{:S(2)}) copy-start(bf16[1,8,2304]{2,1,0:T(8,128)(2,1)} %param.5) | copy-start | bytes 110596
  6.5 94.2 %all-gather.3.cloned.1.call-start = ((), (), s32[]{:S(2)}) async-start(), calls=%async_computation.1 | async-start | bytes 11280384 | tf_op jit(solution)/shard_map/all_gather | solution.py:10
  7.3 141.9 %reduce-scatter.2.cloned.1.call-start = ((), (), s32[]{:S(2)}) async-start(), calls=%async_computation.2 | async-start | bytes 786432 | tf_op jit(solution)/shard_map/reduce_scatter | solution.py:24
Sparse Core Ops, SparseCore 0:
  9.6 91.0 all-gather.2
  137.2 11.8 reduce-scatter.1
where the time goes:
time: 156 us
  waiting for transfers between devices  89.7 us (58%)
  blocking collectives  34.1 us (22%)
  matrix products  16.1 us (10%)
  between operations  14.1 us (9%)
  local copies, waits for them, and re-layouts  2 us (1%)
    all_gather x1, waiting for transfers between devices, on_device(): full_factor = lax.all_gather(factor, 'blk', axis=1, tiled=True)  76.9 us
    all_gather x1, blocking collectives, on_device(): kernel_piece = lax.all_gather(kernel, 'blk', axis=1, tiled=True)  20.3 us
    unnamed x1, blocking collectives  13.8 us
    reduce_scatter x1, waiting for transfers between devices, on_device(): lax.psum_scatter(score_block, 'expert', scatter_dimension=1, tiled=True)  12 us
    dot_general x1, matrix products, on_device(): jnp.einsum('etk,erk->etr', pre_train, full_factor, preferred_element_type...  11.3 us
    dot_general x1, matrix products, on_device(): jnp.einsum('eqk,etk->eqt', query_grads, kernel_piece, preferred_element_t...  4.75 us
  transfers between devices with their start and end apart: 2, of which 2 were waited for; matrix products, arithmetic and copies ran while one was open for 1% of the time, Pallas kernels for 0%

commit v1 on v0

v1 whole, which is shorter than its diff:
```python
import functools

import jax
import jax.numpy as jnp
import numpy as np
from jax import lax
from jax.experimental import pallas as pl
from jax.experimental.pallas import tpu as pltpu
from jax.sharding import PartitionSpec as P

TOKS_EX = 64
MESH = pl.DeviceIdType.MESH
NT = (((1,), (1,)), ((), ()))
CHUNKS = 4


def kernel(
    n_exp, n_chip,
    counts_ref, train_ref, place_ref, query_hbm, factor_hbm, out_ref,
    query, factor, train_out, train_in, part, part_out, part_in,
    pre_out, pre_in, ker, kmat, score, score_in,
    query_sem, own_sem, pair_send, pair_recv,
    a_send, a_recv, b_send, b_recv, c_send, c_recv, d_send, d_recv,
    f_send, f_recv, e_send, e_recv,
):
    expert, blk = lax.axis_index("expert"), lax.axis_index("blk")
    chip, core = blk // 2, blk % 2
    mate = chip * 2 + (1 - core)
    peers = [lax.rem(chip + k, n_chip) for k in range(1, n_chip)]
    rivals = [lax.rem(expert + k, n_exp) for k in range(1, n_exp)]
    t_loc, depth = train_ref.shape[0], factor_hbm.shape[0]
    t_plane = t_loc * n_chip
    wide = 2 * depth

    own_copy = pltpu.make_async_copy(factor_hbm, factor.at[core], own_sem)
    own_copy.start()
    query_copy = pltpu.make_async_copy(query_hbm, query, query_sem)
    query_copy.start()

    barrier = pltpu.get_barrier_semaphore()
    for peer in peers:
        pl.semaphore_signal(barrier, inc=1, device_id=(expert, peer * 2 + core), device_id_type=MESH)
    pl.semaphore_signal(barrier, inc=1, device_id=(expert, mate), device_id_type=MESH)
    for rival in rivals:
        pl.semaphore_signal(barrier, inc=1, device_id=(rival, blk), device_id_type=MESH)

    train = train_ref[...].astype(jnp.float32)
    for c in range(n_chip):
        train_out[c] = train[:, c * wide:(c + 1) * wide].astype(jnp.bfloat16)
    pl.semaphore_wait(barrier, n_chip - 1 + 1 + n_exp - 1)

    def to_peers(source, target, send, recv):
        copies = []
        for k, peer in enumerate(peers):
            copy = pltpu.make_async_remote_copy(
                src_ref=source(peer), dst_ref=target(chip), send_sem=send.at[k],
                recv_sem=recv.at[chip], device_id=(expert, peer * 2 + core), device_id_type=MESH,
            )
            copy.start()
            copies.append(copy)
        return copies

    def from_peer(source, target, send, recv, k):
        peer = peers[k]
        pltpu.make_async_remote_copy(
            src_ref=source(peer), dst_ref=target(peer), send_sem=send.at[k],
            recv_sem=recv.at[peer], device_id=(expert, peer * 2 + core), device_id_type=MESH,
        ).wait_recv()

    a_args = (lambda c: train_out.at[c], lambda c: train_in.at[c], a_send, a_recv)
    a_copies = to_peers(*a_args)
    pair_copy = pltpu.make_async_remote_copy(
        src_ref=factor_hbm, dst_ref=factor.at[core], send_sem=pair_send, recv_sem=pair_recv,
        device_id=(expert, mate), device_id_type=MESH,
    )
    pair_copy.start()
    train_in[chip] = train_out[chip]
    own_copy.wait()
    pair_copy.wait_recv()
    for k in range(n_chip - 1):
        from_peer(*a_args, k)

    rows = train_in[...].astype(jnp.float32).reshape(t_plane, wide)
    first = rows[:, :depth].astype(jnp.bfloat16)
    second = rows[:, depth:].astype(jnp.bfloat16)
    share = jnp.dot(first, factor[0], preferred_element_type=jnp.float32)
    share = share + jnp.dot(second, factor[1], preferred_element_type=jnp.float32)
    share = share.reshape(n_chip, t_loc, share.shape[-1])
    part[...] = share
    part_out[...] = share.astype(jnp.bfloat16)
    b_args = (lambda c: part_out.at[c], lambda c: part_in.at[c], b_send, b_recv)
    b_copies = to_peers(*b_args)
    total = part[chip]
    for k in range(n_chip - 1):
        from_peer(*b_args, k)
        total = total + part_in[peers[k]].astype(jnp.float32)
    at_row = lax.broadcasted_iota(jnp.int32, total.shape, 0)
    weight = jnp.zeros(total.shape, jnp.float32)
    for i in range(t_loc):
        weight = jnp.where(at_row == i, counts_ref[0, i].astype(jnp.float32) / TOKS_EX, weight)
    pre_out[...] = (total * weight).astype(jnp.bfloat16)

    c_args = (lambda c: pre_out, lambda c: pre_in.at[c], c_send, c_recv)
    c_copies = to_peers(*c_args)
    pre_in[chip] = pre_out[...]
    for k in range(n_chip - 1):
        from_peer(*c_args, k)
    pre = pre_in[...].astype(jnp.float32).reshape(t_plane, pre_in.shape[-1]).astype(jnp.bfloat16)
    halves = [
        lax.dot_general(factor[c], pre, NT, preferred_element_type=jnp.float32) for c in range(2)
    ]
    ker[core, chip] = jnp.concatenate(halves, axis=1).astype(jnp.bfloat16)

    d_args = (lambda c: ker.at[core, chip], lambda c: ker.at[core, c], d_send, d_recv)
    d_copies = to_peers(*d_args)
    f_copies = []

    def pass_on(c, k):
        copy = pltpu.make_async_remote_copy(
            src_ref=ker.at[core, c], dst_ref=ker.at[core, c], send_sem=f_send.at[k],
            recv_sem=f_recv.at[c], device_id=(expert, mate), device_id_type=MESH,
        )
        copy.start()
        f_copies.append(copy)

    pass_on(chip, n_chip - 1)
    for k in range(n_chip - 1):
        from_peer(*d_args, k)
        pass_on(peers[k], k)
    for c in range(n_chip):
        pltpu.make_async_remote_copy(
            src_ref=ker.at[1 - core, c], dst_ref=ker.at[1 - core, c], send_sem=f_send.at[c],
            recv_sem=f_recv.at[c], device_id=(expert, mate), device_id_type=MESH,
        ).wait_recv()

    t_all = 2 * t_plane
    for c in range(n_chip):
        both = jnp.concatenate([ker[0, c], ker[1, c]], axis=1)
        placed = jnp.dot(both, place_ref[...], preferred_element_type=jnp.float32).astype(kmat.dtype)
        for half in range(2):
            start = (2 * c + half) * depth
            kmat[start:start + depth, :] = placed[:, half * t_all:(half + 1) * t_all]

    query_copy.wait()
    matrix = kmat[...].astype(jnp.bfloat16)
    side = query.shape[0] // 2
    step = side // CHUNKS
    t_out = t_all // n_exp
    e_copies = []
    for i in range(CHUNKS):
        at = slice(i * step, (i + 1) * step)
        low = jnp.dot(query[at, :], matrix, preferred_element_type=jnp.float32)
        high = jnp.dot(query[side + i * step:side + (i + 1) * step, :], matrix, preferred_element_type=jnp.float32)
        for g in range(n_exp):
            cols = slice(g * t_out, (g + 1) * t_out)
            score[g, i] = jnp.concatenate([low[:, cols], high[:, cols]], axis=1)
        for k, rival in enumerate(rivals):
            copy = pltpu.make_async_remote_copy(
                src_ref=score.at[rival, i], dst_ref=score_in.at[expert, i],
                send_sem=e_send.at[k, i], recv_sem=e_recv.at[expert, i],
                device_id=(rival, blk), device_id_type=MESH,
            )
            copy.start()
            e_copies.append(copy)
    for i in range(CHUNKS):
        total = score[expert, i]
        for k, rival in enumerate(rivals):
            pltpu.make_async_remote_copy(
                src_ref=score.at[rival, i], dst_ref=score_in.at[rival, i],
                send_sem=e_send.at[k, i], recv_sem=e_recv.at[rival, i],
                device_id=(rival, blk), device_id_type=MESH,
            ).wait_recv()
            total = total + score_in[rival, i]
        out_ref[i * step:(i + 1) * step, :] = total
    pair_copy.wait_send()
    for copy in a_copies + b_copies + c_copies + d_copies + f_copies + e_copies:
        copy.wait_send()


def placement(n_chip, t_loc):
    t_plane = n_chip * t_loc
    t_all = 2 * t_plane
    table = np.zeros((2, 2, t_plane, 2, t_all), np.float32)
    for core in range(2):
        for chip in range(n_chip):
            for i in range(t_loc):
                for half in range(2):
                    table[core, half, chip * t_loc + i, half, (2 * chip + core) * t_loc + i] = 1
    return table.reshape(2 * t_all, 2 * t_all)


def on_device(n_exp, n_blk, query_grads, train_grads, counts, factor):
    n_chip = n_blk // 2
    query_grads, train_grads, factor = query_grads[0], train_grads[0], factor[0]
    q_loc, width = query_grads.shape
    t_loc, depth = train_grads.shape[0], factor.shape[0]
    t_plane = t_loc * n_chip
    t_all = 2 * t_plane
    t_out = t_all // n_exp
    bf16, f32 = jnp.bfloat16, jnp.float32
    place = jnp.asarray(placement(n_chip, t_loc), bf16)
    vmem = pl.BlockSpec(memory_space=pltpu.VMEM)
    hbm = pl.BlockSpec(memory_space=pl.ANY)
    dma = pltpu.SemaphoreType.DMA
    side = q_loc // 2
    packed = pl.pallas_call(
        functools.partial(kernel, n_exp, n_chip),
        out_shape=jax.ShapeDtypeStruct((side, 2 * t_out), f32),
        in_specs=[pl.BlockSpec(memory_space=pltpu.SMEM), vmem, vmem, hbm, hbm],
        out_specs=vmem,
        scratch_shapes=[
            pltpu.VMEM((q_loc, width), bf16),
            pltpu.VMEM((2, depth, width), bf16),
            pltpu.VMEM((n_chip, t_loc, 2 * depth), bf16),
            pltpu.VMEM((n_chip, t_loc, 2 * depth), bf16),
            pltpu.VMEM((n_chip, t_loc, width), f32),
            pltpu.VMEM((n_chip, t_loc, width), bf16),
            pltpu.VMEM((n_chip, t_loc, width), bf16),
            pltpu.VMEM((t_loc, width), bf16),
            pltpu.VMEM((n_chip, t_loc, width), bf16),
            pltpu.VMEM((2, n_chip, depth, 2 * t_plane), bf16),
            pltpu.VMEM((width, t_all), bf16 if depth % 16 == 0 else f32),
            pltpu.VMEM((n_exp, CHUNKS, side // CHUNKS, 2 * t_out), f32),
            pltpu.VMEM((n_exp, CHUNKS, side // CHUNKS, 2 * t_out), f32),
            dma, dma, dma, dma,
            dma((n_chip,)), dma((n_chip,)), dma((n_chip,)), dma((n_chip,)),
            dma((n_chip,)), dma((n_chip,)), dma((n_chip,)), dma((n_chip,)),
            dma((n_chip,)), dma((n_chip,)), dma((n_exp, CHUNKS)), dma((n_exp, CHUNKS)),
        ],
        compiler_params=pltpu.CompilerParams(collective_id=0, has_side_effects=True),
        name="influence",
    )(counts, train_grads, place, query_grads, factor)
    return jnp.concatenate([packed[:, :t_out], packed[:, t_out:]], axis=0)


def solution(mesh):
    return jax.shard_map(
        functools.partial(on_device, mesh.shape["expert"], mesh.shape["blk"]),
        mesh=mesh,
        in_specs=(
            P("expert", "blk", None),
            P("expert", "blk", None),
            P("expert", "blk"),
            P("expert", "blk", None),
        ),
        out_specs=P("blk", "expert"),
        check_vma=False,
    )
```

time: 156 us -> 45.8 us (0.29)
  waiting for transfers between devices: 89.7 us -> 0 us
  Pallas kernels: 0 us -> 43.6 us
  blocking collectives: 34.1 us -> 0 us
  matrix products: 16.1 us -> 0 us
  between operations: 14.1 us -> 0.02 us
    all_gather x1 -> x0, waiting for transfers between devices: 76.9 us -> none  [on_device(): full_factor = lax.all_gather(factor, 'blk', axis=1, tiled=True)]
    pallas_call x0 -> x1, Pallas kernels: none -> 43.6 us  [on_device(): pl.pallas_call(functools.partial(kernel, n_exp, n_chip), out_shape=jax.Sh...]
    all_gather x1 -> x0, blocking collectives: 20.3 us -> none  [on_device(): kernel_piece = lax.all_gather(kernel, 'blk', axis=1, tiled=True)]
    dot_general x2 -> x0, matrix products: 16.1 us -> none  [the longest x1 11.3 us: on_device(): jnp.einsum('etk,erk->etr', pre_train, full_factor, preferred_element_type...]
    unnamed x1 -> x0, blocking collectives: 13.8 us -> none
    reduce_scatter x1 -> x0, waiting for transfers between devices: 12 us -> none  [on_device(): lax.psum_scatter(score_block, 'expert', scatter_dimension=1, tiled=True)]
    unnamed x5 -> x0, local copies, waits for them, and re-layouts: 2 us -> none
  transfers between devices with their start and end apart: 2 -> 0, of which waited for: 2 -> 0; matrix products, arithmetic and copies ran while one was open for 1% -> 0% of each run, Pallas kernels for 0% -> 0%
where the time goes in v1:
time: 45.8 us; the launch traced here: 45.7 us
  Pallas kernels  43.6 us (95%)
  local copies, waits for them, and re-layouts  2.04 us (4%)
    pallas_call x1, Pallas kernels, on_device(): pl.pallas_call(functools.partial(kernel, n_exp, n_chip), out_shape=jax.Sh...  43.6 us
    slice x1, local copies, waits for them, and re-layouts, on_device(): return jnp.concatenate([packed[:, :t_out], packed[:, t_out:]], axis=0)  1.15 us

profile of v1, /device:TPU:0, one launch (start us, length us, event | category | flops | bytes accessed | tf_op | source)
XLA Modules:
  0.0 45.7 jit_solution(15922825173546253681)
XLA Ops:
  0.0 43.6 %influence.1 = f32[512,128]{1,0:T(8,128)} custom-call(s32[1,8]{1,0:T(1,128)} %counts_ref.1, bf16[8,2304]{1,0:T(8,128)(2,1)} %bitcast.5, bf16[256,256]{1,0:T(8,128)(2,1)} %constant.2.clone.place_ref, bf16[1024,2304]{1,0:T(8,128)(2,1)} %bitcast.3, bf16[144,2304]{1,0:T(8,128)(2,1)} %bitcast.4), custom_call_target="tpu_custom_call" | custom-call | tf_op jit(solution)/shard_map/influence/pallas_call | solution.py:206
  43.6 1.2 %fusion = (f32[512,64]{1,0:T(8,128)S(1)}, f32[512,64]{1,0:T(8,128)S(1)}) fusion(f32[512,128]{1,0:T(8,128)} %influence.1), kind=kLoop, calls=%fused_computation.1 | loop fusion | bytes 524288 | tf_op jit(solution)/shard_map/slice | solution.py:233
  44.8 0.9 %copy.6 = f32[1024,64]{0,1:T(8,128)} copy(f32[1024,64]{1,0:T(8,128)S(1)} %pad_maximum_fusion) | data formatting | bytes 524288 | tf_op jit(solution)/shard_map/concatenate | solution.py:233
  (1 shorter events, 0.0 us)

commit v2 on v1

--- a/solution.py
+++ b/solution.py
@@ -2,7 +2,6 @@
 
 import jax
 import jax.numpy as jnp
-import numpy as np
 from jax import lax
 from jax.experimental import pallas as pl
 from jax.experimental.pallas import tpu as pltpu
@@ -16,7 +15,7 @@
 
 def kernel(
     n_exp, n_chip,
-    counts_ref, train_ref, place_ref, query_hbm, factor_hbm, out_ref,
+    counts_ref, train_ref, query_hbm, factor_hbm, out_ref,
     query, factor, train_out, train_in, part, part_out, part_in,
     pre_out, pre_in, ker, kmat, score, score_in,
     query_sem, own_sem, pair_send, pair_recv,
@@ -66,6 +65,37 @@
             src_ref=source(peer), dst_ref=target(peer), send_sem=send.at[k],
             recv_sem=recv.at[peer], device_id=(expert, peer * 2 + core), device_id_type=MESH,
         ).wait_recv()
+
+    lines = n_chip // 2
+    line, side_of = chip // 2, chip % 2
+    along = [lax.rem(line + k, lines) * 2 + side_of for k in range(1, lines)]
+    pair = line * 2 + (1 - side_of)
+
+    def gather_copy(source, target, send, recv, k, slot, to):
+        return pltpu.make_async_remote_copy(
+            src_ref=source, dst_ref=target(slot), send_sem=send.at[k], recv_sem=recv.at[slot],
+            device_id=(expert, to * 2 + core), device_id_type=MESH,
+        )
+
+    def gather(source, target, send, recv, landed):
+        copies = []
+        for k, to in enumerate(along):
+            copies.append(gather_copy(source, target, send, recv, k, chip, to))
+        copies.append(gather_copy(source, target, send, recv, lines - 1, chip, pair))
+        for copy in copies:
+            copy.start()
+        landed(chip, 0)
+        for k, other in enumerate(along):
+            gather_copy(source, target, send, recv, k, other, other).wait_recv()
+            copy = gather_copy(target(other), target, send, recv, lines + k, other, pair)
+            copy.start()
+            copies.append(copy)
+            landed(other, 1 + k)
+        for k in range(lines):
+            other = lax.rem(line + k, lines) * 2 + (1 - side_of)
+            gather_copy(source, target, send, recv, k, other, pair).wait_recv()
+            landed(other, lines + k)
+        return copies
 
     a_args = (lambda c: train_out.at[c], lambda c: train_in.at[c], a_send, a_recv)
     a_copies = to_peers(*a_args)
@@ -100,19 +130,14 @@
         weight = jnp.where(at_row == i, counts_ref[0, i].astype(jnp.float32) / TOKS_EX, weight)
     pre_out[...] = (total * weight).astype(jnp.bfloat16)
 
-    c_args = (lambda c: pre_out, lambda c: pre_in.at[c], c_send, c_recv)
-    c_copies = to_peers(*c_args)
+    c_copies = gather(pre_out, lambda c: pre_in.at[c], c_send, c_recv, lambda c, k: None)
     pre_in[chip] = pre_out[...]
-    for k in range(n_chip - 1):
-        from_peer(*c_args, k)
     pre = pre_in[...].astype(jnp.float32).reshape(t_plane, pre_in.shape[-1]).astype(jnp.bfloat16)
     halves = [
         lax.dot_general(factor[c], pre, NT, preferred_element_type=jnp.float32) for c in range(2)
     ]
     ker[core, chip] = jnp.concatenate(halves, axis=1).astype(jnp.bfloat16)
 
-    d_args = (lambda c: ker.at[core, chip], lambda c: ker.at[core, c], d_send, d_recv)
-    d_copies = to_peers(*d_args)
     f_copies = []
 
     def pass_on(c, k):
@@ -123,10 +148,7 @@
         copy.start()
         f_copies.append(copy)
 
-    pass_on(chip, n_chip - 1)
-    for k in range(n_chip - 1):
-        from_peer(*d_args, k)
-        pass_on(peers[k], k)
+    d_copies = gather(ker.at[core, chip], lambda c: ker.at[core, c], d_send, d_recv, pass_on)
     for c in range(n_chip):
         pltpu.make_async_remote_copy(
             src_ref=ker.at[1 - core, c], dst_ref=ker.at[1 - core, c], send_sem=f_send.at[c],
@@ -135,25 +157,25 @@
 
     t_all = 2 * t_plane
     for c in range(n_chip):
-        both = jnp.concatenate([ker[0, c], ker[1, c]], axis=1)
-        placed = jnp.dot(both, place_ref[...], preferred_element_type=jnp.float32).astype(kmat.dtype)
+        even, odd = ker[0, c].astype(jnp.float32), ker[1, c].astype(jnp.float32)
         for half in range(2):
+            cols = slice(half * t_plane, (half + 1) * t_plane)
             start = (2 * c + half) * depth
-            kmat[start:start + depth, :] = placed[:, half * t_all:(half + 1) * t_all]
+            both = jnp.concatenate([even[:, cols], odd[:, cols]], axis=1)
+            kmat[start:start + depth, :] = both.astype(kmat.dtype)
 
     query_copy.wait()
     matrix = kmat[...].astype(jnp.bfloat16)
-    side = query.shape[0] // 2
-    step = side // CHUNKS
+    step = query.shape[0] // CHUNKS
     t_out = t_all // n_exp
     e_copies = []
     for i in range(CHUNKS):
-        at = slice(i * step, (i + 1) * step)
-        low = jnp.dot(query[at, :], matrix, preferred_element_type=jnp.float32)
-        high = jnp.dot(query[side + i * step:side + (i + 1) * step, :], matrix, preferred_element_type=jnp.float32)
-        for g in range(n_exp):
-            cols = slice(g * t_out, (g + 1) * t_out)
-            score[g, i] = jnp.concatenate([low[:, cols], high[:, cols]], axis=1)
+        found = jnp.dot(query[i * step:(i + 1) * step, :], matrix, preferred_element_type=jnp.float32).T
+        for plane in range(2):
+            for c in range(n_chip):
+                start = plane * t_plane + c * t_loc
+                group, row = divmod((2 * c + plane) * t_loc, t_out)
+                score[group, i, row:row + t_loc, :] = found[start:start + t_loc, :]
         for k, rival in enumerate(rivals):
             copy = pltpu.make_async_remote_copy(
                 src_ref=score.at[rival, i], dst_ref=score_in.at[expert, i],
@@ -171,22 +193,10 @@
                 device_id=(rival, blk), device_id_type=MESH,
             ).wait_recv()
             total = total + score_in[rival, i]
-        out_ref[i * step:(i + 1) * step, :] = total
+        out_ref[:, i * step:(i + 1) * step] = total
     pair_copy.wait_send()
     for copy in a_copies + b_copies + c_copies + d_copies + f_copies + e_copies:
         copy.wait_send()
-
-
-def placement(n_chip, t_loc):
-    t_plane = n_chip * t_loc
-    t_all = 2 * t_plane
-    table = np.zeros((2, 2, t_plane, 2, t_all), np.float32)
-    for core in range(2):
-        for chip in range(n_chip):
-            for i in range(t_loc):
-                for half in range(2):
-                    table[core, half, chip * t_loc + i, half, (2 * chip + core) * t_loc + i] = 1
-    return table.reshape(2 * t_all, 2 * t_all)
 
 
 def on_device(n_exp, n_blk, query_grads, train_grads, counts, factor):
@@ -198,15 +208,13 @@
     t_all = 2 * t_plane
     t_out = t_all // n_exp
     bf16, f32 = jnp.bfloat16, jnp.float32
-    place = jnp.asarray(placement(n_chip, t_loc), bf16)
     vmem = pl.BlockSpec(memory_space=pltpu.VMEM)
     hbm = pl.BlockSpec(memory_space=pl.ANY)
     dma = pltpu.SemaphoreType.DMA
-    side = q_loc // 2
-    packed = pl.pallas_call(
+    transposed = pl.pallas_call(
         functools.partial(kernel, n_exp, n_chip),
-        out_shape=jax.ShapeDtypeStruct((side, 2 * t_out), f32),
-        in_specs=[pl.BlockSpec(memory_space=pltpu.SMEM), vmem, vmem, hbm, hbm],
+        out_shape=jax.ShapeDtypeStruct((t_out, q_loc), f32),
+        in_specs=[pl.BlockSpec(memory_space=pltpu.SMEM), vmem, hbm, hbm],
         out_specs=vmem,
         scratch_shapes=[
             pltpu.VMEM((q_loc, width), bf16),
@@ -220,8 +228,8 @@
             pltpu.VMEM((n_chip, t_loc, width), bf16),
             pltpu.VMEM((2, n_chip, depth, 2 * t_plane), bf16),
             pltpu.VMEM((width, t_all), bf16 if depth % 16 == 0 else f32),
-            pltpu.VMEM((n_exp, CHUNKS, side // CHUNKS, 2 * t_out), f32),
-            pltpu.VMEM((n_exp, CHUNKS, side // CHUNKS, 2 * t_out), f32),
+            pltpu.VMEM((n_exp, CHUNKS, t_out, q_loc // CHUNKS), f32),
+            pltpu.VMEM((n_exp, CHUNKS, t_out, q_loc // CHUNKS), f32),
             dma, dma, dma, dma,
             dma((n_chip,)), dma((n_chip,)), dma((n_chip,)), dma((n_chip,)),
             dma((n_chip,)), dma((n_chip,)), dma((n_chip,)), dma((n_chip,)),
@@ -229,8 +237,8 @@
         ],
         compiler_params=pltpu.CompilerParams(collective_id=0, has_side_effects=True),
         name="influence",
-    )(counts, train_grads, place, query_grads, factor)
-    return jnp.concatenate([packed[:, :t_out], packed[:, t_out:]], axis=0)
+    )(counts, train_grads, query_grads, factor)
+    return transposed.T
 
 
 def solution(mesh):

time: 45.8 us -> 47.3 us (1.033)
  Pallas kernels: 43.6 us -> 45.4 us
    pallas_call x1, Pallas kernels: 43.6 us -> 45.4 us  [on_device(): pl.pallas_call(functools.partial(kernel, n_exp, n_chip), out_shape=jax.Sh...]
    unnamed x0 -> x1, local copies, waits for them, and re-layouts: none -> 1.67 us
    slice x1 -> x0, local copies, waits for them, and re-layouts: 1.15 us -> none  [on_device(): return jnp.concatenate([packed[:, :t_out], packed[:, t_out:]], axis=0)]
    concatenate x1 -> x0, local copies, waits for them, and re-layouts: 0.89 us -> none  [on_device(): return jnp.concatenate([packed[:, :t_out], packed[:, t_out:]], axis=0)]
where the time goes in v2:
time: 47.3 us; the launch traced here: 47.1 us
  Pallas kernels  45.4 us (96%)
  local copies, waits for them, and re-layouts  1.67 us (4%)
    pallas_call x1, Pallas kernels, on_device(): pl.pallas_call(functools.partial(kernel, n_exp, n_chip), out_shape=jax.Sh...  45.4 us
    unnamed x1, local copies, waits for them, and re-layouts  1.67 us

profile of v2, /device:TPU:0, one launch (start us, length us, event | category | flops | bytes accessed | tf_op | source)
XLA Modules:
  0.0 47.1 jit_solution(3278819888897716601)
XLA Ops:
  0.0 45.4 %influence.1 = f32[64,1024]{1,0:T(8,128)} custom-call(s32[1,8]{1,0:T(1,128)} %counts_ref.1, bf16[8,2304]{1,0:T(8,128)(2,1)} %bitcast.7, bf16[1024,2304]{1,0:T(8,128)(2,1)} %bitcast.4, bf16[144,2304]{1,0:T(8,128)(2,1)} %bitcast.6), custom_call_target="tpu_custom_call" | custom-call | tf_op jit(solution)/shard_map/influence/pallas_call | solution.py:214
  45.4 1.7 %copy.6 = f32[1024,64]{0,1:T(8,128)} copy(f32[1024,64]{0,1:T(8,128)} %bitcast.5) | data formatting | bytes 524288

commit v3 on v2

--- a/solution.py
+++ b/solution.py
@@ -16,8 +16,8 @@
 def kernel(
     n_exp, n_chip,
     counts_ref, train_ref, query_hbm, factor_hbm, out_ref,
-    query, factor, train_out, train_in, part, part_out, part_in,
-    pre_out, pre_in, ker, kmat, score, score_in,
+    query, factor, train_out, train_in, part, part_out, part_in, near_in,
+    pre_out, pre_in, ker, kmat, score, score_out, score_in,
     query_sem, own_sem, pair_send, pair_recv,
     a_send, a_recv, b_send, b_recv, c_send, c_recv, d_send, d_recv,
     f_send, f_recv, e_send, e_recv,
@@ -66,37 +66,6 @@
             recv_sem=recv.at[peer], device_id=(expert, peer * 2 + core), device_id_type=MESH,
         ).wait_recv()
 
-    lines = n_chip // 2
-    line, side_of = chip // 2, chip % 2
-    along = [lax.rem(line + k, lines) * 2 + side_of for k in range(1, lines)]
-    pair = line * 2 + (1 - side_of)
-
-    def gather_copy(source, target, send, recv, k, slot, to):
-        return pltpu.make_async_remote_copy(
-            src_ref=source, dst_ref=target(slot), send_sem=send.at[k], recv_sem=recv.at[slot],
-            device_id=(expert, to * 2 + core), device_id_type=MESH,
-        )
-
-    def gather(source, target, send, recv, landed):
-        copies = []
-        for k, to in enumerate(along):
-            copies.append(gather_copy(source, target, send, recv, k, chip, to))
-        copies.append(gather_copy(source, target, send, recv, lines - 1, chip, pair))
-        for copy in copies:
-            copy.start()
-        landed(chip, 0)
-        for k, other in enumerate(along):
-            gather_copy(source, target, send, recv, k, other, other).wait_recv()
-            copy = gather_copy(target(other), target, send, recv, lines + k, other, pair)
-            copy.start()
-            copies.append(copy)
-            landed(other, 1 + k)
-        for k in range(lines):
-            other = lax.rem(line + k, lines) * 2 + (1 - side_of)
-            gather_copy(source, target, send, recv, k, other, pair).wait_recv()
-            landed(other, lines + k)
-        return copies
-
     a_args = (lambda c: train_out.at[c], lambda c: train_in.at[c], a_send, a_recv)
     a_copies = to_peers(*a_args)
     pair_copy = pltpu.make_async_remote_copy(
@@ -118,26 +87,44 @@
     share = share.reshape(n_chip, t_loc, share.shape[-1])
     part[...] = share
     part_out[...] = share.astype(jnp.bfloat16)
-    b_args = (lambda c: part_out.at[c], lambda c: part_in.at[c], b_send, b_recv)
-    b_copies = to_peers(*b_args)
+    half_chips = n_chip // 2
+    base = chip // half_chips * half_chips
+    near = [base + lax.rem(chip - base + k, half_chips) for k in range(1, half_chips)]
+    far = [n_chip - half_chips - base + lax.rem(chip - base + k, half_chips) for k in range(half_chips)]
+    order = [(peer, part_out, part_in) for peer in far] + [(peer, part, near_in) for peer in near]
+
+    def share_copy(k, slot, peer, source, target):
+        return pltpu.make_async_remote_copy(
+            src_ref=source.at[peer], dst_ref=target.at[slot], send_sem=b_send.at[k],
+            recv_sem=b_recv.at[slot], device_id=(expert, peer * 2 + core), device_id_type=MESH,
+        )
+
+    b_copies = [share_copy(k, chip, *entry) for k, entry in enumerate(order)]
+    for copy in b_copies:
+        copy.start()
     total = part[chip]
-    for k in range(n_chip - 1):
-        from_peer(*b_args, k)
-        total = total + part_in[peers[k]].astype(jnp.float32)
+    for k, (peer, source, target) in reversed(list(enumerate(order))):
+        share_copy(k, peer, peer, source, target).wait_recv()
+        total = total + target[peer].astype(jnp.float32)
     at_row = lax.broadcasted_iota(jnp.int32, total.shape, 0)
     weight = jnp.zeros(total.shape, jnp.float32)
     for i in range(t_loc):
         weight = jnp.where(at_row == i, counts_ref[0, i].astype(jnp.float32) / TOKS_EX, weight)
     pre_out[...] = (total * weight).astype(jnp.bfloat16)
 
-    c_copies = gather(pre_out, lambda c: pre_in.at[c], c_send, c_recv, lambda c, k: None)
+    c_args = (lambda c: pre_out, lambda c: pre_in.at[c], c_send, c_recv)
+    c_copies = to_peers(*c_args)
     pre_in[chip] = pre_out[...]
+    for k in range(n_chip - 1):
+        from_peer(*c_args, k)
     pre = pre_in[...].astype(jnp.float32).reshape(t_plane, pre_in.shape[-1]).astype(jnp.bfloat16)
     halves = [
         lax.dot_general(factor[c], pre, NT, preferred_element_type=jnp.float32) for c in range(2)
     ]
     ker[core, chip] = jnp.concatenate(halves, axis=1).astype(jnp.bfloat16)
 
+    d_args = (lambda c: ker.at[core, chip], lambda c: ker.at[core, c], d_send, d_recv)
+    d_copies = to_peers(*d_args)
     f_copies = []
 
     def pass_on(c, k):
@@ -148,7 +135,10 @@
         copy.start()
         f_copies.append(copy)
 
-    d_copies = gather(ker.at[core, chip], lambda c: ker.at[core, c], d_send, d_recv, pass_on)
+    pass_on(chip, n_chip - 1)
+    for k in range(n_chip - 1):
+        from_peer(*d_args, k)
+        pass_on(peers[k], k)
     for c in range(n_chip):
         pltpu.make_async_remote_copy(
             src_ref=ker.at[1 - core, c], dst_ref=ker.at[1 - core, c], send_sem=f_send.at[c],
@@ -171,14 +161,19 @@
     e_copies = []
     for i in range(CHUNKS):
         found = jnp.dot(query[i * step:(i + 1) * step, :], matrix, preferred_element_type=jnp.float32).T
-        for plane in range(2):
-            for c in range(n_chip):
+        pieces = []
+        for c in range(n_chip):
+            for plane in range(2):
                 start = plane * t_plane + c * t_loc
-                group, row = divmod((2 * c + plane) * t_loc, t_out)
-                score[group, i, row:row + t_loc, :] = found[start:start + t_loc, :]
+                pieces.append(found[start:start + t_loc, :])
+        ordered = jnp.concatenate(pieces, axis=0)
+        for g in range(n_exp):
+            block = ordered[g * t_out:(g + 1) * t_out, :]
+            score[g, i] = block
+            score_out[g, i] = block.astype(jnp.bfloat16)
         for k, rival in enumerate(rivals):
             copy = pltpu.make_async_remote_copy(
-                src_ref=score.at[rival, i], dst_ref=score_in.at[expert, i],
+                src_ref=score_out.at[rival, i], dst_ref=score_in.at[expert, i],
                 send_sem=e_send.at[k, i], recv_sem=e_recv.at[expert, i],
                 device_id=(rival, blk), device_id_type=MESH,
             )
@@ -188,11 +183,11 @@
         total = score[expert, i]
         for k, rival in enumerate(rivals):
             pltpu.make_async_remote_copy(
-                src_ref=score.at[rival, i], dst_ref=score_in.at[rival, i],
+                src_ref=score_out.at[rival, i], dst_ref=score_in.at[rival, i],
                 send_sem=e_send.at[k, i], recv_sem=e_recv.at[rival, i],
                 device_id=(rival, blk), device_id_type=MESH,
             ).wait_recv()
-            total = total + score_in[rival, i]
+            total = total + score_in[rival, i].astype(jnp.float32)
         out_ref[:, i * step:(i + 1) * step] = total
     pair_copy.wait_send()
     for copy in a_copies + b_copies + c_copies + d_copies + f_copies + e_copies:
@@ -224,12 +219,14 @@
             pltpu.VMEM((n_chip, t_loc, width), f32),
             pltpu.VMEM((n_chip, t_loc, width), bf16),
             pltpu.VMEM((n_chip, t_loc, width), bf16),
+            pltpu.VMEM((n_chip, t_loc, width), f32),
             pltpu.VMEM((t_loc, width), bf16),
             pltpu.VMEM((n_chip, t_loc, width), bf16),
             pltpu.VMEM((2, n_chip, depth, 2 * t_plane), bf16),
             pltpu.VMEM((width, t_all), bf16 if depth % 16 == 0 else f32),
             pltpu.VMEM((n_exp, CHUNKS, t_out, q_loc // CHUNKS), f32),
-            pltpu.VMEM((n_exp, CHUNKS, t_out, q_loc // CHUNKS), f32),
+            pltpu.VMEM((n_exp, CHUNKS, t_out, q_loc // CHUNKS), bf16),
+            pltpu.VMEM((n_exp, CHUNKS, t_out, q_loc // CHUNKS), bf16),
             dma, dma, dma, dma,
             dma((n_chip,)), dma((n_chip,)), dma((n_chip,)), dma((n_chip,)),
             dma((n_chip,)), dma((n_chip,)), dma((n_chip,)), dma((n_chip,)),

time: 47.3 us -> 42 us (0.89)
  Pallas kernels: 45.4 us -> 40.1 us
    pallas_call x1, Pallas kernels: 45.4 us -> 40.1 us  [on_device(): pl.pallas_call(functools.partial(kernel, n_exp, n_chip), out_shape=jax.Sh...]
where the time goes in v3:
time: 42 us; the launch traced here: 41.8 us
  Pallas kernels  40.1 us (95%)
  local copies, waits for them, and re-layouts  1.67 us (4%)
    pallas_call x1, Pallas kernels, on_device(): pl.pallas_call(functools.partial(kernel, n_exp, n_chip), out_shape=jax.Sh...  40.1 us
    unnamed x1, local copies, waits for them, and re-layouts  1.67 us

profile of v3, /device:TPU:0, one launch (start us, length us, event | category | flops | bytes accessed | tf_op | source)
XLA Modules:
  0.0 41.8 jit_solution(14762427807593377989)
XLA Ops:
  0.0 40.1 %influence.1 = f32[64,1024]{1,0:T(8,128)} custom-call(s32[1,8]{1,0:T(1,128)} %counts_ref.1, bf16[8,2304]{1,0:T(8,128)(2,1)} %bitcast.7, bf16[1024,2304]{1,0:T(8,128)(2,1)} %bitcast.4, bf16[144,2304]{1,0:T(8,128)(2,1)} %bitcast.6), custom_call_target="tpu_custom_call" | custom-call | tf_op jit(solution)/shard_map/influence/pallas_call | solution.py:209
  40.1 1.7 %copy.6 = f32[1024,64]{0,1:T(8,128)} copy(f32[1024,64]{0,1:T(8,128)} %bitcast.5) | data formatting | bytes 524288
